TPU v7x, 32 devices: a whole 2x2x4 slice. The times are simulated.
32 devices in a mesh: dp: 8 (over z, x), seq: 4 (over y, core).
Axes of the slice: x: 2, y: 2, z: 4, core: 2. Of those that a mesh axis runs over, the one named last changes fastest.
Arguments:
- field: bfloat16 [8, 2048, 1024], P('dp', 'seq'), may hold values from -6 to 6
- eq_embed: bfloat16 [8, 512, 1024], P('dp', 'seq'), may hold values from -6 to 6
- eq_len: int32 [8], replicated, may hold values from 1 to 512, 2048 in all
- owner: int32 [8], replicated, may hold values from 0 to 7, as said below
- norm_gain: float32 [1024], replicated, may hold values from 0.1 to 1.9
- w_qkv: bfloat16 [1024, 3072], replicated, may hold values from -0.176776695 to 0.176776695
- w_out: bfloat16 [1024, 1024], replicated, may hold values from -0.1875 to 0.1875
- cross_gain: float32 [1024], replicated, may hold values from 0.1 to 1.9
- w_cq: bfloat16 [1024, 1024], replicated, may hold values from -0.125 to 0.125
- w_ckv: bfloat16 [1024, 2048], replicated, may hold values from -0.125 to 0.125
- w_cout: bfloat16 [1024, 1024], replicated, may hold values from -0.1875 to 0.1875
Outputs:
- joined: bfloat16 [8, 2048, 1024], P('dp', 'seq')
Inputs may be any that keep to these rules, and one draw needn't show every extreme that they name: `owner`: every slot number appears exactly once. `eq_len`: some slot has all 512 tokens real.
All inputs are finite; a program needn't handle non-finite values.
Results may differ from a plain program's by a relative error of at most 0.0055.
Values may be sent and summed in bfloat16 or wider, within the bound.
A program may use at most 128 MiB of HBM per device.

v0:
```python
import jax
import jax.numpy as jnp
from jax import lax
from jax.sharding import PartitionSpec as P

D = 1024
HEADS = 16
HEAD_DIM = 64


def normalize(values, gain):
    return values * lax.rsqrt(jnp.mean(values * values, axis=-1, keepdims=True) + 1e-06) * gain


def attend(query, keys, values, valid):
    rows = query.shape[0]
    heads = query.shape[1]
    depth = query.shape[2]
    block = min(512, rows)
    scale = depth ** (-0.5)

    def one_block(query_block):
        scores = (
            jnp.einsum("qhd,khd->hqk", query_block, keys, preferred_element_type=jnp.float32)
            * scale
        )
        expo = jnp.where(valid[None, None, :], jnp.exp(scores), 0.0)
        weights = (expo / jnp.sum(expo, axis=-1, keepdims=True)).astype(jnp.bfloat16)
        return jnp.einsum(
            "hqk,khd->qhd", weights, values, preferred_element_type=jnp.float32
        ).astype(jnp.bfloat16)

    blocks = lax.map(one_block, query.reshape(rows // block, block, heads, depth))
    return blocks.reshape(rows, heads * depth)


def pick_slot(wanted, carry, piece):
    inside = (wanted >= 0) & (wanted < piece.shape[0])
    picked = lax.dynamic_index_in_dim(
        piece, jnp.clip(wanted, 0, piece.shape[0] - 1), 0, keepdims=False
    )
    return jnp.where(inside, picked, carry)


def per_device(
    field, eq_embed, eq_len, owner, norm_gain, w_qkv, w_out, cross_gain, w_cq, w_ckv, w_cout
):
    tokens = field[0].astype(jnp.float32)
    tok_rows = tokens.shape[0]
    groups = lax.axis_size("seq")
    head_count = HEADS // groups
    normed = normalize(tokens, norm_gain).astype(jnp.bfloat16)
    projected = jnp.dot(normed, w_qkv, preferred_element_type=jnp.float32).astype(jnp.bfloat16)
    stacked = projected.reshape(tok_rows, 3, D)
    local_heads = lax.all_to_all(stacked, "seq", split_axis=2, concat_axis=0, tiled=True)
    seq_rows = local_heads.shape[0]
    split = local_heads.reshape(seq_rows, 3, head_count, HEAD_DIM)
    every = jnp.ones((seq_rows,), dtype=bool)
    attended = attend(split[:, 0], split[:, 1], split[:, 2], every)
    merged = lax.all_to_all(attended, "seq", split_axis=0, concat_axis=1, tiled=True)
    mixed = tokens + jnp.dot(merged, w_out, preferred_element_type=jnp.float32)
    cross_in = normalize(mixed, cross_gain).astype(jnp.bfloat16)
    cross_q = jnp.dot(cross_in, w_cq, preferred_element_type=jnp.float32).astype(jnp.bfloat16)
    slot = lax.dynamic_index_in_dim(owner, lax.axis_index("dp"), 0, keepdims=False)
    length = lax.dynamic_index_in_dim(eq_len, slot, 0, keepdims=False)
    eq_rows = eq_embed.shape[1]
    empty = jnp.zeros(eq_embed.shape[1:], jnp.bfloat16)
    owned_rows = pick_slot(slot, empty, lax.all_gather(eq_embed, "dp", axis=0, tiled=True))
    owned_kv = jnp.dot(owned_rows, w_ckv, preferred_element_type=jnp.float32).astype(jnp.bfloat16)
    whole_kv = lax.all_gather(owned_kv, "seq", axis=0, tiled=True)
    whole_kv = whole_kv.reshape(eq_rows * groups, 2, HEADS, HEAD_DIM)
    valid = jnp.arange(eq_rows * groups, dtype=jnp.int32) < length
    cross_att = attend(
        cross_q.reshape(tok_rows, HEADS, HEAD_DIM), whole_kv[:, 0], whole_kv[:, 1], valid
    )
    joined = mixed + jnp.dot(cross_att, w_cout, preferred_element_type=jnp.float32)
    return joined.astype(jnp.bfloat16)[None]


def solution(mesh):
    in_specs = (
        P("dp", "seq", None),
        P("dp", "seq", None),
        P(),
        P(),
        P(),
        P(),
        P(),
        P(),
        P(),
        P(),
        P(),
    )
    out_specs = P("dp", "seq", None)
    return jax.shard_map(
        per_device, mesh=mesh, in_specs=in_specs, out_specs=out_specs, check_vma=False
    )
```

profile of v0, /device:TPU:0, one launch (start us, length us, event | category | flops | bytes accessed | tf_op | source)
XLA Modules:
  0.0 189.4 jit_solution(14081409868850262506)
XLA Ops:
  8.8 8.3 %convolution_convert_fusion = bf16[512,3072]{1,0:T(8,128)(2,1)} fusion(bf16[1024,3072]{1,0:T(8,128)(2,1)} %param.18, bf16[1,512,1024]{2,1,0:T(8,128)(2,1)} %param.13, f32[1024]{0:T(1024)} %param.17, f32[512]{0:T(512)S(1)} %add_rsqrt_fusion.1), kind=kOutput, calls=%fused_computation.16 | convolution fusion | flops 3224895488 | bytes 10491904 | tf_op jit(solution)/shard_map/dot_general | solution.py:53
  17.1 4.7 %copy.28 = bf16[512,3072]{0,1:T(8,128)(2,1)} copy(bf16[512,3072]{1,0:T(8,128)(2,1)} %convolution_convert_fusion) | data formatting | bytes 6291456 | tf_op jit(solution)/shard_map/convert_element_type | solution.py:53
  21.7 6.5 %copy.29 = bf16[512,3,1024]{0,1,2:T(4,128)(2,1)} copy(bf16[512,3,1024]{0,2,1:T(8,128)(2,1)} %bitcast.75) | data formatting | bytes 6291456 | tf_op jit(solution)/shard_map/reshape | solution.py:54
  28.3 5.0 %all-to-all-start = ((bf16[512,3,1024]{0,1,2:T(4,128)(2,1)}), bf16[512,3,1024]{0,1,2:T(4,128)(2,1)}, u32[]{:S(2)}, u32[]{:S(2)}) async-start(bf16[512,3,1024]{0,1,2:T(4,128)(2,1)} %copy.29), calls=%async_computation | async-start | bytes 8388608 | tf_op jit(solution)/shard_map/all_to_all | solution.py:55
  35.8 46.4 %all-to-all-done = bf16[512,3,1024]{0,1,2:T(4,128)(2,1)} async-done(((bf16[512,3,1024]{0,1,2:T(4,128)(2,1)}), bf16[512,3,1024]{0,1,2:T(4,128)(2,1)}, u32[]{:S(2)}, u32[]{:S(2)}) %all-to-all-start) | async-done | bytes 3145760 | tf_op jit(solution)/shard_map/all_to_all | solution.py:55
  82.2 3.0 %copy.30 = bf16[512,3,1024]{0,2,1:T(8,128)(2,1)S(1)} copy(bf16[512,3,1024]{0,1,2:T(4,128)(2,1)} %all-to-all-done) | data formatting | bytes 6291456 | tf_op jit(solution)/shard_map/all_to_all | solution.py:55
  85.1 4.1 %copy.31 = bf16[4,512,3,256]{1,0,3,2:T(4,128)(2,1)} copy(bf16[4,512,3,256]{1,3,0,2:T(8,128)(2,1)S(1)} %bitcast.76) | data formatting | bytes 6291456 | tf_op jit(solution)/shard_map/all_to_all | solution.py:55
  89.2 6.1 %reshape.50 = bf16[2048,3,4,64]{0,3,2,1:T(8,128)(2,1)} reshape(bf16[4,512,3,256]{1,0,3,2:T(4,128)(2,1)} %copy.31) | data formatting | bytes 6291456 | tf_op jit(solution)/shard_map/reshape | solution.py:57
  95.3 3.6 %slice_bitcast_fusion.4 = (bf16[2048,4,64]{0,2,1:T(8,128)(2,1)}, bf16[2048,4,64]{0,2,1:T(8,128)(2,1)S(1)}, bf16[2048,1,4,64]{0,3,2,1:T(8,128)(2,1)}) fusion(bf16[2048,3,4,64]{0,3,2,1:T(8,128)(2,1)} %reshape.50), kind=kLoop, calls=%fused_computation.33 | loop fusion | bytes 6291456 | tf_op jit(solution)/shard_map/squeeze | solution.py:59
  103.9 3.8 %convolution_convert_fusion.1 = bf16[128,2048]{1,0:T(8,128)(2,1)} fusion(bf16[1024,2048]{1,0:T(8,128)(2,1)} %param.22, bf16[8,128,1024]{2,1,0:T(8,128)(2,1)} %all-gather.3.cloned.1.call-done, s32[]{:T(128)S(6)} %min.4, pred[]{:T(512)S(6)} %and.4), kind=kOutput, calls=%fused_computation.20 | convolution fusion | flops 537264128 | bytes 4980741 | tf_op jit(solution)/shard_map/dot_general | solution.py:69
  107.8 33.5 %while.2 = (s32[]{:T(128)}, bf16[4,512,4,64]{1,3,2,0:T(8,128)(2,1)}, bf16[4,512,4,64]{1,3,2,0:T(8,128)(2,1)}, bf16[2048,4,64]{0,2,1:T(8,128)(2,1)S(1)}, bf16[2048,4,64]{0,2,1:T(8,128)(2,1)}, /*index=5*/s32[]{:T(128)}) while((s32[]{:T(128)}, bf16[4,512,4,64]{1,3,2,0:T(8,128)(2,1)}, bf16[4,512,4,64]{1,3,2,0:T(8,128)(2,1)}, ...), condition=%wide.region_3.4_spmd, body=%wide.region_1.3_spmd.sunk | while | flops 1094842368 | bytes 40386672 | solution.py:33
  107.8 4.0 %fusion.49 = (f32[4,512]{1,0:T(4,128)S(1)}, f32[4,512,2048]{2,1,0:T(8,128)S(1)}) fusion(bf16[2048,4,64]{0,2,1:T(8,128)(2,1)S(1)} %get-tuple-element.135, bf16[4,512,4,64]{1,3,2,0:T(8,128)(2,1)} %get-tuple-element.134, s32[]{:T(128)S(6)} %copy.40), kind=kOutput, calls=%fused_computation.2.clone.1 | convolution fusion | flops 545257472 | bytes 18096132 | tf_op jit(solution)/shard_map/while/body/eval_jaxpr/qhd,khd->hqk/dot_general | solution.py:24
  111.9 4.3 %fusion.50 = bf16[4,512,4,64]{1,3,2,0:T(8,128)(2,1)} fusion(bf16[4,512,4,64]{1,3,2,0:T(8,128)(2,1)} %get-tuple-element.127, s32[]{:T(128)S(6)} %copy.40, bf16[2048,4,64]{0,2,1:T(8,128)(2,1)S(1)} %copy-done.4, f32[4,512,2048]{2,1,0:T(8,128)S(1)} %get-tuple-element.118, f32[4,512]{1,0:T(4,128)S(1)} %get-tuple-element.119), kind=kOutput, calls=%fused_computation.6.clone.1 | convolution fusion | flops 549584896 | bytes 18096132 | tf_op jit(solution)/shard_map/while/body/eval_jaxpr/hqk,khd->qhd/dot_general | solution.py:29
  116.2 4.1 %fusion.49 = (f32[4,512]{1,0:T(4,128)S(1)}, f32[4,512,2048]{2,1,0:T(8,128)S(1)}) fusion(bf16[2048,4,64]{0,2,1:T(8,128)(2,1)S(1)} %get-tuple-element.135, bf16[4,512,4,64]{1,3,2,0:T(8,128)(2,1)} %get-tuple-element.134, s32[]{:T(128)S(6)} %copy.40), kind=kOutput, calls=%fused_computation.2.clone.1 | convolution fusion | flops 545257472 | bytes 18096132 | tf_op jit(solution)/shard_map/while/body/eval_jaxpr/qhd,khd->hqk/dot_general | solution.py:24
  120.3 4.3 %fusion.50 = bf16[4,512,4,64]{1,3,2,0:T(8,128)(2,1)} fusion(bf16[4,512,4,64]{1,3,2,0:T(8,128)(2,1)} %get-tuple-element.127, s32[]{:T(128)S(6)} %copy.40, bf16[2048,4,64]{0,2,1:T(8,128)(2,1)S(1)} %copy-done.4, f32[4,512,2048]{2,1,0:T(8,128)S(1)} %get-tuple-element.118, f32[4,512]{1,0:T(4,128)S(1)} %get-tuple-element.119), kind=kOutput, calls=%fused_computation.6.clone.1 | convolution fusion | flops 549584896 | bytes 18096132 | tf_op jit(solution)/shard_map/while/body/eval_jaxpr/hqk,khd->qhd/dot_general | solution.py:29
  124.6 4.0 %fusion.49 = (f32[4,512]{1,0:T(4,128)S(1)}, f32[4,512,2048]{2,1,0:T(8,128)S(1)}) fusion(bf16[2048,4,64]{0,2,1:T(8,128)(2,1)S(1)} %get-tuple-element.135, bf16[4,512,4,64]{1,3,2,0:T(8,128)(2,1)} %get-tuple-element.134, s32[]{:T(128)S(6)} %copy.40), kind=kOutput, calls=%fused_computation.2.clone.1 | convolution fusion | flops 545257472 | bytes 18096132 | tf_op jit(solution)/shard_map/while/body/eval_jaxpr/qhd,khd->hqk/dot_general | solution.py:24
  128.6 4.3 %fusion.50 = bf16[4,512,4,64]{1,3,2,0:T(8,128)(2,1)} fusion(bf16[4,512,4,64]{1,3,2,0:T(8,128)(2,1)} %get-tuple-element.127, s32[]{:T(128)S(6)} %copy.40, bf16[2048,4,64]{0,2,1:T(8,128)(2,1)S(1)} %copy-done.4, f32[4,512,2048]{2,1,0:T(8,128)S(1)} %get-tuple-element.118, f32[4,512]{1,0:T(4,128)S(1)} %get-tuple-element.119), kind=kOutput, calls=%fused_computation.6.clone.1 | convolution fusion | flops 549584896 | bytes 18096132 | tf_op jit(solution)/shard_map/while/body/eval_jaxpr/hqk,khd->qhd/dot_general | solution.py:29
  132.9 4.0 %fusion.49 = (f32[4,512]{1,0:T(4,128)S(1)}, f32[4,512,2048]{2,1,0:T(8,128)S(1)}) fusion(bf16[2048,4,64]{0,2,1:T(8,128)(2,1)S(1)} %get-tuple-element.135, bf16[4,512,4,64]{1,3,2,0:T(8,128)(2,1)} %get-tuple-element.134, s32[]{:T(128)S(6)} %copy.40), kind=kOutput, calls=%fused_computation.2.clone.1 | convolution fusion | flops 545257472 | bytes 18096132 | tf_op jit(solution)/shard_map/while/body/eval_jaxpr/qhd,khd->hqk/dot_general | solution.py:24
  137.0 4.3 %fusion.50 = bf16[4,512,4,64]{1,3,2,0:T(8,128)(2,1)} fusion(bf16[4,512,4,64]{1,3,2,0:T(8,128)(2,1)} %get-tuple-element.127, s32[]{:T(128)S(6)} %copy.40, bf16[2048,4,64]{0,2,1:T(8,128)(2,1)S(1)} %copy-done.4, f32[4,512,2048]{2,1,0:T(8,128)S(1)} %get-tuple-element.118, f32[4,512]{1,0:T(4,128)S(1)} %get-tuple-element.119), kind=kOutput, calls=%fused_computation.6.clone.1 | convolution fusion | flops 549584896 | bytes 18096132 | tf_op jit(solution)/shard_map/while/body/eval_jaxpr/hqk,khd->qhd/dot_general | solution.py:29
  141.3 3.7 %all-to-all-start.1 = ((bf16[4,512,256]{1,2,0:T(8,128)(2,1)}), bf16[4,512,256]{1,2,0:T(8,128)(2,1)S(1)}, u32[]{:S(2)}, u32[]{:S(2)}) async-start(bf16[4,512,256]{1,2,0:T(8,128)(2,1)} %bitcast.80), calls=%async_computation.1 | async-start | bytes 2097152 | tf_op jit(solution)/shard_map/all_to_all | solution.py:60
  148.0 11.3 %all-to-all-done.1 = bf16[4,512,256]{1,2,0:T(8,128)(2,1)S(1)} async-done(((bf16[4,512,256]{1,2,0:T(8,128)(2,1)}), bf16[4,512,256]{1,2,0:T(8,128)(2,1)S(1)}, u32[]{:S(2)}, u32[]{:S(2)}) %all-to-all-start.1) | async-done | bytes 1048608 | tf_op jit(solution)/shard_map/all_to_all | solution.py:60
  167.1 3.9 %copy.33 = bf16[512,2048]{0,1:T(8,128)(2,1)} copy(bf16[512,2048]{1,0:T(8,128)(2,1)} %all-gather.5.cloned.1.call-done) | data formatting | bytes 4194304 | tf_op jit(solution)/shard_map/all_gather | solution.py:70
  171.0 5.5 %fusion.10 = (f32[16,512]{1,0:T(8,128)S(1)}, f32[16,512,512]{1,2,0:T(8,128)S(1)}) fusion(pred[512]{0:T(512)(128)(4,1)S(1)} %iota_compare_fusion, bf16[512,16,64]{0,2,1:T(8,128)(2,1)S(1)} %bitcast.81, bf16[512,2,16,64]{0,3,2,1:T(8,128)(2,1)} %bitcast.78), kind=kOutput, calls=%fused_computation.14 | convolution fusion | flops 549445632 | bytes 18907648 | tf_op jit(solution)/shard_map/while/body/eval_jaxpr/qhd,khd->hqk/dot_general | solution.py:24
  176.6 3.7 %fusion.15 = bf16[16,64,512]{2,1,0:T(8,128)(2,1)S(1)} fusion(f32[16,512,512]{1,2,0:T(8,128)S(1)} %get-tuple-element.84, f32[16,512]{1,0:T(8,128)S(1)} %get-tuple-element.83, pred[512]{0:T(512)(128)(4,1)S(1)} %iota_compare_fusion, bf16[512,2,16,64]{0,3,2,1:T(8,128)(2,1)S(1)} %bitcast.79), kind=kOutput, calls=%fused_computation.27 | convolution fusion | flops 554172416 | bytes 18907648 | tf_op jit(solution)/shard_map/while/body/eval_jaxpr/hqk,khd->qhd/dot_general | solution.py:29
  (45 shorter events, 19.5 us)
Async XLA Ops:
  6.5 152.7 %copy-start = (bf16[1024,1024]{1,0:T(8,128)(2,1)S(1)}, bf16[1024,1024]{1,0:T(8,128)(2,1)}, u32[]{:S(2)}) copy-start(bf16[1024,1024]{1,0:T(8,128)(2,1)} %param.19) | copy-start | bytes 6291460
  6.5 97.4 %all-gather.3.cloned.1.call-start = ((), (), s32[]{:S(2)}) async-start(), calls=%async_computation.2 | async-start | bytes 2359296 | tf_op jit(solution)/shard_map/all_gather | solution.py:68
  28.3 5.2 %copy-start.8 = (s32[8]{0:T(128)S(1)}, s32[8]{0:T(128)}, u32[]{:S(2)}) copy-start(s32[8]{0:T(128)} %param.16) | copy-start | bytes 100
  28.3 53.9 %all-to-all-start = ((bf16[512,3,1024]{0,1,2:T(4,128)(2,1)}), bf16[512,3,1024]{0,1,2:T(4,128)(2,1)}, u32[]{:S(2)}, u32[]{:S(2)}) async-start(bf16[512,3,1024]{0,1,2:T(4,128)(2,1)} %copy.29), calls=%async_computation | async-start | bytes 8388608 | tf_op jit(solution)/shard_map/all_to_all | solution.py:55
  33.3 133.8 %all-gather.5.cloned.1.call-start = ((), (), s32[]{:S(2)}) async-start(), calls=%async_computation.3 | async-start | bytes 2621440 | tf_op jit(solution)/shard_map/all_gather | solution.py:70
  107.8 38.9 %copy-start.9 = (s32[8]{0:T(128)S(1)}, s32[8]{0:T(128)}, u32[]{:S(2)}) copy-start(s32[8]{0:T(128)} %param.15) | copy-start | bytes 100
  107.8 4.1 %copy-start.4 = (bf16[2048,4,64]{0,2,1:T(8,128)(2,1)S(1)}, bf16[2048,4,64]{0,2,1:T(8,128)(2,1)}, u32[]{:S(2)}) copy-start(bf16[2048,4,64]{0,2,1:T(8,128)(2,1)} %get-tuple-element.136) | copy-start | bytes 3145732 | tf_op jit(solution)/shard_map/while
  116.2 4.1 %copy-start.4 = (bf16[2048,4,64]{0,2,1:T(8,128)(2,1)S(1)}, bf16[2048,4,64]{0,2,1:T(8,128)(2,1)}, u32[]{:S(2)}) copy-start(bf16[2048,4,64]{0,2,1:T(8,128)(2,1)} %get-tuple-element.136) | copy-start | bytes 3145732 | tf_op jit(solution)/shard_map/while
  124.6 4.0 %copy-start.4 = (bf16[2048,4,64]{0,2,1:T(8,128)(2,1)S(1)}, bf16[2048,4,64]{0,2,1:T(8,128)(2,1)}, u32[]{:S(2)}) copy-start(bf16[2048,4,64]{0,2,1:T(8,128)(2,1)} %get-tuple-element.136) | copy-start | bytes 3145732 | tf_op jit(solution)/shard_map/while
  132.9 4.0 %copy-start.4 = (bf16[2048,4,64]{0,2,1:T(8,128)(2,1)S(1)}, bf16[2048,4,64]{0,2,1:T(8,128)(2,1)}, u32[]{:S(2)}) copy-start(bf16[2048,4,64]{0,2,1:T(8,128)(2,1)} %get-tuple-element.136) | copy-start | bytes 3145732 | tf_op jit(solution)/shard_map/while
  141.3 18.0 %all-to-all-start.1 = ((bf16[4,512,256]{1,2,0:T(8,128)(2,1)}), bf16[4,512,256]{1,2,0:T(8,128)(2,1)S(1)}, u32[]{:S(2)}, u32[]{:S(2)}) async-start(bf16[4,512,256]{1,2,0:T(8,128)(2,1)} %bitcast.80), calls=%async_computation.1 | async-start | bytes 2097152 | tf_op jit(solution)/shard_map/all_to_all | solution.py:60
  159.2 4.1 %copy-start.5 = (bf16[1024,1024]{1,0:T(8,128)(2,1)S(1)}, bf16[1024,1024]{1,0:T(8,128)(2,1)}, u32[]{:S(2)}) copy-start(bf16[1024,1024]{1,0:T(8,128)(2,1)} %param.21) | copy-start | bytes 6291460
  159.2 4.1 %copy-start.7 = (f32[1024]{0:T(1024)S(1)}, f32[1024]{0:T(1024)}, u32[]{:S(2)}) copy-start(f32[1024]{0:T(1024)} %param.20) | copy-start | bytes 12292
  162.0 1.3 copy-start.1
  171.0 5.5 %copy-start.3 = (bf16[512,2048]{0,1:T(8,128)(2,1)S(1)}, bf16[512,2048]{0,1:T(8,128)(2,1)}, u32[]{:S(2)}) copy-start(bf16[512,2048]{0,1:T(8,128)(2,1)} %copy.33) | copy-start | bytes 6291460
  176.6 3.8 %copy-start.2 = (f32[512,1024]{1,0:T(8,128)S(1)}, f32[512,1024]{1,0:T(8,128)}, u32[]{:S(2)}) copy-start(f32[512,1024]{1,0:T(8,128)} %copy-done.1) | copy-start | bytes 6291460
  176.6 3.8 %copy-start.6 = (bf16[1024,1024]{1,0:T(8,128)(2,1)S(1)}, bf16[1024,1024]{1,0:T(8,128)(2,1)}, u32[]{:S(2)}) copy-start(bf16[1024,1024]{1,0:T(8,128)(2,1)} %param.23) | copy-start | bytes 6291460
Sparse Core Ops, SparseCore 0:
  9.5 51.9 all-gather.2
  107.9 23.6 all-gather.4
where the time goes:
time: 190 us; the launch traced here: 189 us
  matrix products  62 us (33%)
  waiting for transfers between devices  58.4 us (31%)
  local copies, waits for them, and re-layouts  41 us (22%)
  between operations  16.9 us (9%)
  starting transfers between devices  8.93 us (5%)
  other arithmetic  2.16 us (1%)
    all_to_all x1, waiting for transfers between devices, per_device(): lax.all_to_all(stacked, 'seq', split_axis=2, concat_axis=0, tiled=True)  46.4 us
    dot_general x5, matrix products, one_block(): jnp.einsum('qhd,khd->hqk', query_block, keys, preferred_element_type=jnp....  21.7 us
    dot_general x5, matrix products, one_block(): jnp.einsum('hqk,khd->qhd', weights, values, preferred_element_type=jnp.fl...  20.9 us
    all_to_all x1, waiting for transfers between devices, per_device(): lax.all_to_all(attended, 'seq', split_axis=0, concat_axis=1, tiled=True)  11.3 us
    dot_general x1, matrix products, per_device(): jnp.dot(normed, w_qkv, preferred_element_type=jnp.float32)  8.28 us
    all_to_all x2, local copies, waits for them, and re-layouts, per_device(): lax.all_to_all(stacked, 'seq', split_axis=2, concat_axis=0, tiled=True)  7.07 us
    reshape x1, local copies, waits for them, and re-layouts, per_device(): stacked = projected.reshape(tok_rows, 3, D)  6.53 us
    reshape x1, local copies, waits for them, and re-layouts, per_device(): split = local_heads.reshape(seq_rows, 3, head_count, HEAD_DIM)  6.1 us
  transfers between devices with their start and end apart: 4, of which 2 were waited for; matrix products, arithmetic and copies ran while one was open for 45% of the time, Pallas kernels for 0%

commit v1 on v0

--- a/solution.py
+++ b/solution.py
@@ -6,6 +6,28 @@
 D = 1024
 HEADS = 16
 HEAD_DIM = 64
+
+
+def in_order(blocks, dim):
+    blocks = jnp.moveaxis(blocks, 0, dim)
+    lengths = blocks.shape
+    return blocks.reshape(*lengths[:dim], lengths[dim] * lengths[dim + 1], *lengths[dim + 2 :])
+
+
+def collected_by_bits(x, axis):
+    length = lax.axis_size(axis)
+    pieces = x[None]
+    for level in range(length.bit_length() - 1):
+        apart = 1 << level
+        theirs = lax.ppermute(pieces, axis, [(i, i ^ apart) for i in range(length)])
+        both = jnp.stack([pieces, theirs])
+        upper = lax.axis_index(axis) >> level & 1
+        pieces = jnp.where(upper == 0, both, both[::-1]).reshape(-1, *x.shape)
+    return pieces
+
+
+def collect(x, axis, dim):
+    return in_order(collected_by_bits(x, axis), dim)
 
 
 def normalize(values, gain):
@@ -67,7 +89,7 @@
     empty = jnp.zeros(eq_embed.shape[1:], jnp.bfloat16)
     owned_rows = pick_slot(slot, empty, lax.all_gather(eq_embed, "dp", axis=0, tiled=True))
     owned_kv = jnp.dot(owned_rows, w_ckv, preferred_element_type=jnp.float32).astype(jnp.bfloat16)
-    whole_kv = lax.all_gather(owned_kv, "seq", axis=0, tiled=True)
+    whole_kv = collect(owned_kv, "seq", 0)
     whole_kv = whole_kv.reshape(eq_rows * groups, 2, HEADS, HEAD_DIM)
     valid = jnp.arange(eq_rows * groups, dtype=jnp.int32) < length
     cross_att = attend(

time: 190 us -> 216 us (1.14)
  waiting for transfers between devices: 58.4 us -> 66.8 us
  local copies, waits for them, and re-layouts: 41 us -> 48.4 us
  other arithmetic: 2.16 us -> 8.49 us
  starting transfers between devices: 8.93 us -> 11.4 us
    ppermute x0 -> x2, waiting for transfers between devices: none -> 13.3 us  [collected_by_bits(): theirs = lax.ppermute(pieces, axis, [(i, i ^ apart) for i in range(length)])]
    select_n x0 -> x1, local copies, waits for them, and re-layouts: none -> 6.14 us  [collected_by_bits(): pieces = jnp.where(upper == 0, both, both[::-1]).reshape(-1, *x.shape)]
    another operation x0 -> x3, other arithmetic: none -> 4.44 us  [collected_by_bits(): both = jnp.stack([pieces, theirs])]
    another operation x0 -> x1, local copies, waits for them, and re-layouts: none -> 4.22 us  [per_device(): whole_kv = whole_kv.reshape(eq_rows * groups, 2, HEADS, HEAD_DIM)]
    all_gather x1 -> x0, local copies, waits for them, and re-layouts: 3.93 us -> none  [per_device(): whole_kv = lax.all_gather(owned_kv, 'seq', axis=0, tiled=True)]
    all_to_all x1, waiting for transfers between devices: 46.4 us -> 43.5 us  [per_device(): lax.all_to_all(stacked, 'seq', split_axis=2, concat_axis=0, tiled=True)]
  transfers between devices with their start and end apart: 4 -> 5, of which waited for: 2 -> 3; matrix products, arithmetic and copies ran while one was open for 45% -> 41% of each run, Pallas kernels for 0% -> 0%
where the time goes in v1:
time: 216 us; the launch traced here: 215 us
  waiting for transfers between devices  66.8 us (31%)
  matrix products  62 us (29%)
  local copies, waits for them, and re-layouts  48.4 us (22%)
  between operations  17.7 us (8%)
  starting transfers between devices  11.4 us (5%)
  other arithmetic  8.49 us (4%)
    all_to_all x1, waiting for transfers between devices, per_device(): lax.all_to_all(stacked, 'seq', split_axis=2, concat_axis=0, tiled=True)  43.5 us
    dot_general x5, matrix products, one_block(): jnp.einsum('qhd,khd->hqk', query_block, keys, preferred_element_type=jnp....  21.6 us
    dot_general x5, matrix products, one_block(): jnp.einsum('hqk,khd->qhd', weights, values, preferred_element_type=jnp.fl...  20.9 us
    ppermute x2, waiting for transfers between devices, collected_by_bits(): theirs = lax.ppermute(pieces, axis, [(i, i ^ apart) for i in range(length)])  13.3 us
    all_to_all x1, waiting for transfers between devices, per_device(): lax.all_to_all(attended, 'seq', split_axis=0, concat_axis=1, tiled=True)  9.28 us
    dot_general x1, matrix products, per_device(): jnp.dot(normed, w_qkv, preferred_element_type=jnp.float32)  8.3 us
    all_to_all x2, local copies, waits for them, and re-layouts, per_device(): lax.all_to_all(stacked, 'seq', split_axis=2, concat_axis=0, tiled=True)  7.09 us
    reshape x1, local copies, waits for them, and re-layouts, per_device(): stacked = projected.reshape(tok_rows, 3, D)  6.55 us
  transfers between devices with their start and end apart: 5, of which 3 were waited for; matrix products, arithmetic and copies ran while one was open for 41% of the time, Pallas kernels for 0%

profile of v1, /device:TPU:0, one launch (start us, length us, event | category | flops | bytes accessed | tf_op | source)
XLA Modules:
  0.0 214.8 jit_solution(14275817892199602792)
XLA Ops:
  8.8 8.3 %convolution_convert_fusion = bf16[512,3072]{1,0:T(8,128)(2,1)} fusion(bf16[1024,3072]{1,0:T(8,128)(2,1)} %param.18, bf16[1,512,1024]{2,1,0:T(8,128)(2,1)} %param.13, f32[1024]{0:T(1024)} %param.17, f32[512]{0:T(512)S(1)} %add_rsqrt_fusion.1), kind=kOutput, calls=%fused_computation.16 | convolution fusion | flops 3224895488 | bytes 10491904 | tf_op jit(solution)/shard_map/dot_general | solution.py:75
  17.1 4.7 %copy.28 = bf16[512,3072]{0,1:T(8,128)(2,1)} copy(bf16[512,3072]{1,0:T(8,128)(2,1)} %convolution_convert_fusion) | data formatting | bytes 6291456 | tf_op jit(solution)/shard_map/convert_element_type | solution.py:75
  21.8 6.6 %copy.29 = bf16[512,3,1024]{0,1,2:T(4,128)(2,1)} copy(bf16[512,3,1024]{0,2,1:T(8,128)(2,1)} %bitcast.84) | data formatting | bytes 6291456 | tf_op jit(solution)/shard_map/reshape | solution.py:76
  28.3 5.2 %all-to-all-start = ((bf16[512,3,1024]{0,1,2:T(4,128)(2,1)}), bf16[512,3,1024]{0,1,2:T(4,128)(2,1)}, u32[]{:S(2)}, u32[]{:S(2)}) async-start(bf16[512,3,1024]{0,1,2:T(4,128)(2,1)} %copy.29), calls=%async_computation | async-start | bytes 8388608 | tf_op jit(solution)/shard_map/all_to_all | solution.py:77
  39.0 43.5 %all-to-all-done = bf16[512,3,1024]{0,1,2:T(4,128)(2,1)} async-done(((bf16[512,3,1024]{0,1,2:T(4,128)(2,1)}), bf16[512,3,1024]{0,1,2:T(4,128)(2,1)}, u32[]{:S(2)}, u32[]{:S(2)}) %all-to-all-start) | async-done | bytes 3145760 | tf_op jit(solution)/shard_map/all_to_all | solution.py:77
  85.4 4.1 %copy.31 = bf16[4,512,3,256]{1,0,3,2:T(4,128)(2,1)} copy(bf16[4,512,3,256]{1,3,0,2:T(8,128)(2,1)S(1)} %bitcast.85) | data formatting | bytes 6291456 | tf_op jit(solution)/shard_map/all_to_all | solution.py:77
  89.5 6.1 %reshape.50 = bf16[2048,3,4,64]{0,3,2,1:T(8,128)(2,1)} reshape(bf16[4,512,3,256]{1,0,3,2:T(4,128)(2,1)} %copy.31) | data formatting | bytes 6291456 | tf_op jit(solution)/shard_map/reshape | solution.py:79
  104.3 3.8 %convolution_convert_fusion.1 = bf16[128,2048]{1,0:T(8,128)(2,1)} fusion(bf16[1024,2048]{1,0:T(8,128)(2,1)} %param.22, bf16[8,128,1024]{2,1,0:T(8,128)(2,1)} %all-gather.2.cloned.1.call-done, s32[]{:T(128)S(6)} %min.4, pred[]{:T(512)S(6)} %and.13), kind=kOutput, calls=%fused_computation.21 | convolution fusion | flops 537264128 | bytes 4980741 | tf_op jit(solution)/shard_map/dot_general | solution.py:91
  108.1 33.4 %while.2 = (s32[]{:T(128)}, bf16[4,512,4,64]{1,3,2,0:T(8,128)(2,1)}, bf16[4,512,4,64]{1,3,2,0:T(8,128)(2,1)}, bf16[2048,4,64]{0,2,1:T(8,128)(2,1)S(1)}, bf16[2048,4,64]{0,2,1:T(8,128)(2,1)}, /*index=5*/s32[]{:T(128)}) while((s32[]{:T(128)}, bf16[4,512,4,64]{1,3,2,0:T(8,128)(2,1)}, bf16[4,512,4,64]{1,3,2,0:T(8,128)(2,1)}, ...), condition=%wide.region_3.4_spmd, body=%wide.region_1.3_spmd.sunk | while | flops 1094842368 | bytes 40386672 | solution.py:55
  108.1 4.0 %fusion.51 = (f32[4,512]{1,0:T(4,128)S(1)}, f32[4,512,2048]{2,1,0:T(8,128)S(1)}) fusion(bf16[2048,4,64]{0,2,1:T(8,128)(2,1)S(1)} %get-tuple-element.137, bf16[4,512,4,64]{1,3,2,0:T(8,128)(2,1)} %get-tuple-element.136, s32[]{:T(128)S(6)} %copy.40), kind=kOutput, calls=%fused_computation.2.clone.1 | convolution fusion | flops 545257472 | bytes 18096132 | tf_op jit(solution)/shard_map/while/body/eval_jaxpr/qhd,khd->hqk/dot_general | solution.py:46
  112.2 4.3 %fusion.52 = bf16[4,512,4,64]{1,3,2,0:T(8,128)(2,1)} fusion(bf16[4,512,4,64]{1,3,2,0:T(8,128)(2,1)} %get-tuple-element.129, s32[]{:T(128)S(6)} %copy.40, bf16[2048,4,64]{0,2,1:T(8,128)(2,1)S(1)} %copy-done.7, f32[4,512,2048]{2,1,0:T(8,128)S(1)} %get-tuple-element.120, f32[4,512]{1,0:T(4,128)S(1)} %get-tuple-element.121), kind=kOutput, calls=%fused_computation.6.clone.1 | convolution fusion | flops 549584896 | bytes 18096132 | tf_op jit(solution)/shard_map/while/body/eval_jaxpr/hqk,khd->qhd/dot_general | solution.py:51
  116.5 4.0 %fusion.51 = (f32[4,512]{1,0:T(4,128)S(1)}, f32[4,512,2048]{2,1,0:T(8,128)S(1)}) fusion(bf16[2048,4,64]{0,2,1:T(8,128)(2,1)S(1)} %get-tuple-element.137, bf16[4,512,4,64]{1,3,2,0:T(8,128)(2,1)} %get-tuple-element.136, s32[]{:T(128)S(6)} %copy.40), kind=kOutput, calls=%fused_computation.2.clone.1 | convolution fusion | flops 545257472 | bytes 18096132 | tf_op jit(solution)/shard_map/while/body/eval_jaxpr/qhd,khd->hqk/dot_general | solution.py:46
  120.5 4.3 %fusion.52 = bf16[4,512,4,64]{1,3,2,0:T(8,128)(2,1)} fusion(bf16[4,512,4,64]{1,3,2,0:T(8,128)(2,1)} %get-tuple-element.129, s32[]{:T(128)S(6)} %copy.40, bf16[2048,4,64]{0,2,1:T(8,128)(2,1)S(1)} %copy-done.7, f32[4,512,2048]{2,1,0:T(8,128)S(1)} %get-tuple-element.120, f32[4,512]{1,0:T(4,128)S(1)} %get-tuple-element.121), kind=kOutput, calls=%fused_computation.6.clone.1 | convolution fusion | flops 549584896 | bytes 18096132 | tf_op jit(solution)/shard_map/while/body/eval_jaxpr/hqk,khd->qhd/dot_general | solution.py:51
  124.8 4.0 %fusion.51 = (f32[4,512]{1,0:T(4,128)S(1)}, f32[4,512,2048]{2,1,0:T(8,128)S(1)}) fusion(bf16[2048,4,64]{0,2,1:T(8,128)(2,1)S(1)} %get-tuple-element.137, bf16[4,512,4,64]{1,3,2,0:T(8,128)(2,1)} %get-tuple-element.136, s32[]{:T(128)S(6)} %copy.40), kind=kOutput, calls=%fused_computation.2.clone.1 | convolution fusion | flops 545257472 | bytes 18096132 | tf_op jit(solution)/shard_map/while/body/eval_jaxpr/qhd,khd->hqk/dot_general | solution.py:46
  128.9 4.3 %fusion.52 = bf16[4,512,4,64]{1,3,2,0:T(8,128)(2,1)} fusion(bf16[4,512,4,64]{1,3,2,0:T(8,128)(2,1)} %get-tuple-element.129, s32[]{:T(128)S(6)} %copy.40, bf16[2048,4,64]{0,2,1:T(8,128)(2,1)S(1)} %copy-done.7, f32[4,512,2048]{2,1,0:T(8,128)S(1)} %get-tuple-element.120, f32[4,512]{1,0:T(4,128)S(1)} %get-tuple-element.121), kind=kOutput, calls=%fused_computation.6.clone.1 | convolution fusion | flops 549584896 | bytes 18096132 | tf_op jit(solution)/shard_map/while/body/eval_jaxpr/hqk,khd->qhd/dot_general | solution.py:51
  133.2 4.0 %fusion.51 = (f32[4,512]{1,0:T(4,128)S(1)}, f32[4,512,2048]{2,1,0:T(8,128)S(1)}) fusion(bf16[2048,4,64]{0,2,1:T(8,128)(2,1)S(1)} %get-tuple-element.137, bf16[4,512,4,64]{1,3,2,0:T(8,128)(2,1)} %get-tuple-element.136, s32[]{:T(128)S(6)} %copy.40), kind=kOutput, calls=%fused_computation.2.clone.1 | convolution fusion | flops 545257472 | bytes 18096132 | tf_op jit(solution)/shard_map/while/body/eval_jaxpr/qhd,khd->hqk/dot_general | solution.py:46
  137.2 4.3 %fusion.52 = bf16[4,512,4,64]{1,3,2,0:T(8,128)(2,1)} fusion(bf16[4,512,4,64]{1,3,2,0:T(8,128)(2,1)} %get-tuple-element.129, s32[]{:T(128)S(6)} %copy.40, bf16[2048,4,64]{0,2,1:T(8,128)(2,1)S(1)} %copy-done.7, f32[4,512,2048]{2,1,0:T(8,128)S(1)} %get-tuple-element.120, f32[4,512]{1,0:T(4,128)S(1)} %get-tuple-element.121), kind=kOutput, calls=%fused_computation.6.clone.1 | convolution fusion | flops 549584896 | bytes 18096132 | tf_op jit(solution)/shard_map/while/body/eval_jaxpr/hqk,khd->qhd/dot_general | solution.py:51
  141.5 4.5 %all-to-all-start.1 = ((bf16[4,512,256]{1,2,0:T(8,128)(2,1)}), bf16[4,512,256]{1,2,0:T(8,128)(2,1)}, u32[]{:S(2)}, u32[]{:S(2)}) async-start(bf16[4,512,256]{1,2,0:T(8,128)(2,1)} %bitcast.86), calls=%async_computation.1 | async-start | bytes 2097152 | tf_op jit(solution)/shard_map/all_to_all | solution.py:82
  151.5 9.3 %all-to-all-done.1 = bf16[4,512,256]{1,2,0:T(8,128)(2,1)} async-done(((bf16[4,512,256]{1,2,0:T(8,128)(2,1)}), bf16[4,512,256]{1,2,0:T(8,128)(2,1)}, u32[]{:S(2)}, u32[]{:S(2)}) %all-to-all-start.1) | async-done | bytes 1048608 | tf_op jit(solution)/shard_map/all_to_all | solution.py:82
  169.4 13.3 %collective-permute-done.1 = bf16[2,128,2048]{2,1,0:T(8,128)(2,1)} collective-permute-done((bf16[2,128,2048]{2,1,0:T(8,128)(2,1)}, bf16[2,128,2048]{2,1,0:T(8,128)(2,1)}, u32[]{:S(2)}, u32[]{:S(2)}) %collective-permute-start.1) | collective-permute-done | bytes 1048608 | tf_op jit(solution)/shard_map/ppermute | solution.py:22
  186.0 6.1 %copy.33 = bf16[2,2,128,2048]{2,1,0,3:T(2,128)(2,1)} copy(bf16[2,2,128,2048]{3,2,1,0:T(8,128)(2,1)} %reverse_select_fusion) | data formatting | bytes 4194304 | tf_op jit(solution)/shard_map/jit(_where)/select_n | solution.py:25
  192.2 4.2 %reshape_reshape_reshape.3 = bf16[512,2,16,64]{0,3,2,1:T(8,128)(2,1)} reshape(bf16[2,2,128,2048]{2,1,0,3:T(2,128)(2,1)} %copy.33) | data formatting | bytes 4194304 | tf_op jit(solution)/shard_map/reshape;reshape;reshape | solution.py:93
  196.4 5.5 %fusion.10 = (f32[16,512]{1,0:T(8,128)S(1)}, f32[16,512,512]{1,2,0:T(8,128)S(1)}) fusion(pred[512]{0:T(512)(128)(4,1)S(1)} %iota_compare_fusion, bf16[512,16,64]{0,2,1:T(8,128)(2,1)S(1)} %bitcast.87, bf16[512,2,16,64]{0,3,2,1:T(8,128)(2,1)} %reshape_reshape_reshape.3), kind=kOutput, calls=%fused_computation.14 | convolution fusion | flops 549445632 | bytes 18907648 | tf_op jit(solution)/shard_map/while/body/eval_jaxpr/qhd,khd->hqk/dot_general | solution.py:46
  202.0 3.7 %fusion.15 = bf16[16,64,512]{2,1,0:T(8,128)(2,1)S(1)} fusion(f32[16,512,512]{1,2,0:T(8,128)S(1)} %get-tuple-element.86, f32[16,512]{1,0:T(8,128)S(1)} %get-tuple-element.85, pred[512]{0:T(512)(128)(4,1)S(1)} %iota_compare_fusion, bf16[512,2,16,64]{0,3,2,1:T(8,128)(2,1)S(1)} %copy-done.5), kind=kOutput, calls=%fused_computation.30 | convolution fusion | flops 554172416 | bytes 18907648 | tf_op jit(solution)/shard_map/while/body/eval_jaxpr/hqk,khd->qhd/dot_general | solution.py:51
  (57 shorter events, 34.8 us)
Async XLA Ops:
  6.5 154.2 %copy-start = (bf16[1024,1024]{1,0:T(8,128)(2,1)S(1)}, bf16[1024,1024]{1,0:T(8,128)(2,1)}, u32[]{:S(2)}) copy-start(bf16[1024,1024]{1,0:T(8,128)(2,1)} %param.19) | copy-start | bytes 6291460
  6.5 97.7 %all-gather.2.cloned.1.call-start = ((), (), s32[]{:S(2)}) async-start(), calls=%async_computation.2 | async-start | bytes 2359296 | tf_op jit(solution)/shard_map/all_gather | solution.py:90
  28.3 5.2 %copy-start.11 = (s32[8]{0:T(128)S(1)}, s32[8]{0:T(128)}, u32[]{:S(2)}) copy-start(s32[8]{0:T(128)} %param.16) | copy-start | bytes 100
  28.3 10.0 %copy-start.12 = (s32[8]{0:T(128)S(1)}, s32[8]{0:T(128)}, u32[]{:S(2)}) copy-start(s32[8]{0:T(128)} %param.15) | copy-start | bytes 100
  28.3 54.1 %all-to-all-start = ((bf16[512,3,1024]{0,1,2:T(4,128)(2,1)}), bf16[512,3,1024]{0,1,2:T(4,128)(2,1)}, u32[]{:S(2)}, u32[]{:S(2)}) async-start(bf16[512,3,1024]{0,1,2:T(4,128)(2,1)} %copy.29), calls=%async_computation | async-start | bytes 8388608 | tf_op jit(solution)/shard_map/all_to_all | solution.py:77
  108.1 37.9 %collective-permute-start = (bf16[1,128,2048]{2,1,0:T(8,128)(2,1)}, bf16[1,128,2048]{2,1,0:T(8,128)(2,1)}, u32[]{:S(2)}, u32[]{:S(2)}) collective-permute-start(bf16[1,128,2048]{2,1,0:T(8,128)(2,1)} %bitcast.16), channel_id=1, source_target_pairs={{0,1},{1,0},{2,3},{3,2},{4,5},{5,4},{6,7},{7,6},{8,9},{9,8},{10,11... | collective-permute-start | bytes 1572872 | tf_op jit(solution)/shard_map/ppermute | solution.py:22
  108.1 4.0 %copy-start.7 = (bf16[2048,4,64]{0,2,1:T(8,128)(2,1)S(1)}, bf16[2048,4,64]{0,2,1:T(8,128)(2,1)}, u32[]{:S(2)}) copy-start(bf16[2048,4,64]{0,2,1:T(8,128)(2,1)} %get-tuple-element.138) | copy-start | bytes 3145732 | tf_op jit(solution)/shard_map/while
  116.5 4.0 %copy-start.7 = (bf16[2048,4,64]{0,2,1:T(8,128)(2,1)S(1)}, bf16[2048,4,64]{0,2,1:T(8,128)(2,1)}, u32[]{:S(2)}) copy-start(bf16[2048,4,64]{0,2,1:T(8,128)(2,1)} %get-tuple-element.138) | copy-start | bytes 3145732 | tf_op jit(solution)/shard_map/while
  124.8 4.0 %copy-start.7 = (bf16[2048,4,64]{0,2,1:T(8,128)(2,1)S(1)}, bf16[2048,4,64]{0,2,1:T(8,128)(2,1)}, u32[]{:S(2)}) copy-start(bf16[2048,4,64]{0,2,1:T(8,128)(2,1)} %get-tuple-element.138) | copy-start | bytes 3145732 | tf_op jit(solution)/shard_map/while
  133.2 4.0 %copy-start.7 = (bf16[2048,4,64]{0,2,1:T(8,128)(2,1)S(1)}, bf16[2048,4,64]{0,2,1:T(8,128)(2,1)}, u32[]{:S(2)}) copy-start(bf16[2048,4,64]{0,2,1:T(8,128)(2,1)} %get-tuple-element.138) | copy-start | bytes 3145732 | tf_op jit(solution)/shard_map/while
  141.5 19.2 %all-to-all-start.1 = ((bf16[4,512,256]{1,2,0:T(8,128)(2,1)}), bf16[4,512,256]{1,2,0:T(8,128)(2,1)}, u32[]{:S(2)}, u32[]{:S(2)}) async-start(bf16[4,512,256]{1,2,0:T(8,128)(2,1)} %bitcast.86), calls=%async_computation.1 | async-start | bytes 2097152 | tf_op jit(solution)/shard_map/all_to_all | solution.py:82
  146.0 14.8 %copy-start.1 = (bf16[1,512,1024]{2,1,0:T(8,128)(2,1)S(1)}, bf16[1,512,1024]{2,1,0:T(8,128)(2,1)}, u32[]{:S(2)}) copy-start(bf16[1,512,1024]{2,1,0:T(8,128)(2,1)} %param.13) | copy-start | bytes 3145732
  149.0 33.7 %collective-permute-start.1 = (bf16[2,128,2048]{2,1,0:T(8,128)(2,1)}, bf16[2,128,2048]{2,1,0:T(8,128)(2,1)}, u32[]{:S(2)}, u32[]{:S(2)}) collective-permute-start(bf16[2,128,2048]{2,1,0:T(8,128)(2,1)} %get-tuple-element.82), channel_id=1, source_target_pairs={{0,2},{1,3},{2,0},{3,1},{4,6},{5,7},{6,4},{7,5},{8,10},{9,11},{10,... | collective-permute-start | bytes 3145736 | tf_op jit(solution)/shard_map/ppermute | solution.py:22
  160.8 4.1 %copy-start.8 = (bf16[1024,1024]{1,0:T(8,128)(2,1)S(1)}, bf16[1024,1024]{1,0:T(8,128)(2,1)}, u32[]{:S(2)}) copy-start(bf16[1024,1024]{1,0:T(8,128)(2,1)} %param.21) | copy-start | bytes 6291460
  160.8 4.1 %copy-start.10 = (f32[1024]{0:T(1024)S(1)}, f32[1024]{0:T(1024)}, u32[]{:S(2)}) copy-start(f32[1024]{0:T(1024)} %param.20) | copy-start | bytes 12292
  163.5 1.3 copy-start.3
  164.9 17.9 %copy-start.2 = (bf16[1,2,128,2048]{3,2,1,0:T(8,128)(2,1)S(1)}, bf16[1,2,128,2048]{3,2,1,0:T(8,128)(2,1)}, u32[]{:S(2)}) copy-start(bf16[1,2,128,2048]{3,2,1,0:T(8,128)(2,1)} %get-tuple-element.81) | copy-start | bytes 3145732
  192.2 4.2 %copy-start.6 = (bf16[512,1024]{0,1:T(8,128)(2,1)S(1)}, bf16[512,1024]{0,1:T(8,128)(2,1)}, u32[]{:S(2)}) copy-start(bf16[512,1024]{0,1:T(8,128)(2,1)} %copy.34) | copy-start | bytes 3145732
  196.4 5.5 %copy-start.5 = (bf16[512,2,16,64]{0,3,2,1:T(8,128)(2,1)S(1)}, bf16[512,2,16,64]{0,3,2,1:T(8,128)(2,1)}, u32[]{:S(2)}) copy-start(bf16[512,2,16,64]{0,3,2,1:T(8,128)(2,1)} %reshape_reshape_reshape.3) | copy-start | bytes 6291460
  201.9 3.8 %copy-start.4 = (f32[512,1024]{1,0:T(8,128)S(1)}, f32[512,1024]{1,0:T(8,128)}, u32[]{:S(2)}) copy-start(f32[512,1024]{1,0:T(8,128)} %copy-done.3) | copy-start | bytes 6291460
  201.9 3.8 %copy-start.9 = (bf16[1024,1024]{1,0:T(8,128)(2,1)S(1)}, bf16[1024,1024]{1,0:T(8,128)(2,1)}, u32[]{:S(2)}) copy-start(bf16[1024,1024]{1,0:T(8,128)(2,1)} %param.23) | copy-start | bytes 6291460
Sparse Core Ops, SparseCore 0:
  9.5 51.9 all-gather.1
